TPU v7x, 256 devices: a whole 4x4x8 slice. The times are simulated.
256 devices in a mesh: chan: 64 (over y, z, core), hour: 4 (over x).
Axes of the slice: x: 4, y: 4, z: 8, core: 2. Of those that a mesh axis runs over, the one named last changes fastest.
Arguments:
- spectra: bfloat16 [8, 2, 8192, 2560], P('hour', None, 'chan'), may hold values from -34 to 34, as said below
- partner_lists: int32 [64, 4], replicated, may hold values from -1 to 63, as said below
- partner_counts: int32 [64], replicated, may hold values from 2 to 4, as said below
Outputs:
- stacks: float32 [256, 8, 128, 256], P(('chan', 'hour'))
Inputs may be any that keep to these rules, and one draw needn't show every extreme that they name: The spectra are finite and bounded. `partner_lists`: row s lists distinct channel blocks, the first being s itself; entries from position partner_counts[s] on are -1. Within their counts, every block is listed by at most 4 rows, and some block by exactly 4. `partner_counts`: some row has exactly 4 partners.
All inputs are finite; a program needn't handle non-finite values.
Results may differ from a plain program's by a relative error of at most 0.0046.
Values may be sent and summed in bfloat16 or wider, within the bound.
A program may use at most 128 MiB of HBM per device.

v0:
```python
import math
import jax
import jax.numpy as jnp
from jax import lax
from jax.sharding import PartitionSpec as P

VS = 8
F0 = 64
NWIN = 8192
SMOOTH = 129
LAGS = 256


def whiten(real_part, imag_part):
    amplitude = jnp.sqrt(real_part * real_part + imag_part * imag_part)
    window_shape = (1,) * (amplitude.ndim - 1) + (SMOOTH,)
    padding = ((0, 0),) * (amplitude.ndim - 1) + ((SMOOTH // 2, SMOOTH // 2),)
    summed = lax.reduce_window(
        amplitude,
        jnp.zeros((), amplitude.dtype),
        lax.add,
        window_shape,
        (1,) * amplitude.ndim,
        padding,
    )
    denominator = summed / SMOOTH + 1e-06
    return (
        (real_part / denominator).astype(jnp.bfloat16),
        (imag_part / denominator).astype(jnp.bfloat16),
    )


def lag_table(band_bins):
    freq_index = jnp.arange(band_bins, dtype=jnp.int32)[:, None] + F0
    lag_index = jnp.arange(LAGS, dtype=jnp.int32)[None, :] - LAGS // 2
    lag_index = jnp.where(lag_index < 0, lag_index + NWIN, lag_index)
    phase_index = freq_index * lag_index % NWIN
    phase_angle = phase_index.astype(jnp.float32) * (2.0 * math.pi / NWIN)
    return jnp.concatenate([jnp.cos(phase_angle), -jnp.sin(phase_angle)], 0).astype(jnp.bfloat16)


def slot_onehot(partner_lists, partner_counts, receiver):
    offsets = jnp.arange(partner_lists.shape[1], dtype=jnp.int32)
    listed = (offsets[None, :] < partner_counts[:, None]) & (partner_lists == receiver)
    member = jnp.any(listed, axis=1)
    slot_rank = jnp.cumsum(member.astype(jnp.int32)) - 1
    slots = jnp.arange(partner_lists.shape[1], dtype=jnp.int32)
    return member[None, :] & (slot_rank[None, :] == slots[:, None])


def shards(spectra, partner_lists, partner_counts):
    windows, _, block_chans, band_bins = spectra.shape
    block_count = lax.axis_size("chan")
    hour_count = lax.axis_size("hour")
    values = spectra.astype(jnp.float32)
    white_re, white_im = whiten(values[:, 0], values[:, 1])
    stride = block_chans // VS
    local_sources = jnp.stack([white_re[:, ::stride, :], white_im[:, ::stride, :]], 1)
    local_sources = jnp.transpose(local_sources, (2, 0, 1, 3))
    receiver = lax.axis_index("chan")
    onehot = slot_onehot(partner_lists, partner_counts, receiver).astype(jnp.bfloat16)
    slot_total = onehot.shape[0]
    gathered = lax.all_gather(local_sources, "chan", axis=0, tiled=True)
    flattened = gathered.reshape(block_count, -1)
    chosen = jnp.dot(onehot, flattened, preferred_element_type=jnp.float32)
    chosen = chosen.reshape(slot_total, VS, windows, 2, band_bins)
    table_values = lag_table(band_bins)
    norm_scale = 1.0 / math.sqrt(4.0 * band_bins * windows * hour_count)

    def one_slot(source):
        cross_re = jnp.zeros((VS, block_chans, band_bins), jnp.float32)
        cross_im = jnp.zeros((VS, block_chans, band_bins), jnp.float32)
        for window in range(windows):
            src_real = source[:, window, 0][:, None, :]
            src_imag = source[:, window, 1][:, None, :]
            recv_real = white_re[window][None, :, :]
            recv_imag = white_im[window][None, :, :]
            cross_re = cross_re + src_real * recv_real + src_imag * recv_imag
            cross_im = cross_im + src_imag * recv_real - src_real * recv_imag
        cross = (
            jnp.concatenate([cross_re, cross_im], -1)
            .astype(jnp.bfloat16)
            .reshape(VS * block_chans, 2 * band_bins)
        )
        lagged = jnp.dot(cross, table_values, preferred_element_type=jnp.float32) * norm_scale
        return lagged.reshape(VS, block_chans, LAGS)

    partial_stacks = lax.map(one_slot, chosen)
    summed_hours = lax.psum(partial_stacks, "hour")
    share = slot_total // hour_count
    return lax.dynamic_slice_in_dim(summed_hours, lax.axis_index("hour") * share, share, 0)


def solution(mesh):
    return jax.shard_map(
        shards,
        mesh=mesh,
        in_specs=(P("hour", None, "chan", None), P(), P()),
        out_specs=P(("chan", "hour"), None, None, None),
        check_vma=False,
    )
```

profile of v0, /device:TPU:1, one launch (start us, length us, event | category | flops | bytes accessed | tf_op | source)
XLA Modules:
  0.0 464.1 jit_solution(17760751546049418316)
XLA Ops:
  6.5 3.2 copy.26
  10.1 2.3 copy-done
  13.3 129.2 %reduce_window.7 = f32[2,128,2560]{1,2,0:T(8,128)} reduce-window(f32[2,128,2560]{1,2,0:T(8,128)S(1)} %add_sqrt_fusion, f32[]{:T(128)} %constant.29.clone.1), window={size=1x1x129 pad=0_0x0_0x64_64}, to_apply=%region_2.0 | reduce-window | flops 83886080 | bytes 5242884 | tf_op jit(solution)/shard_map/reduce_window | solution.py:18
  142.4 4.0 divide_convert_fusion.1
  146.4 10.4 %slice.38 = bf16[2,8,2560]{1,2,0:T(8,128)(2,1)} slice(bf16[2,128,2560]{1,2,0:T(8,128)(2,1)S(1)} %get-tuple-element.90), slice={[0:2:1], [0:128:16], [0:2560:1]} | slice | bytes 163840 | tf_op jit(solution)/shard_map/slice | solution.py:58
  156.8 10.2 %slice.39 = bf16[2,8,2560]{1,2,0:T(8,128)(2,1)} slice(bf16[2,128,2560]{1,2,0:T(8,128)(2,1)S(1)} %get-tuple-element.91), slice={[0:2:1], [0:128:16], [0:2560:1]} | slice | bytes 163840 | tf_op jit(solution)/shard_map/slice | solution.py:58
  167.0 3.8 maximum_bitcast_fusion
  170.8 3.5 copy.27
  177.1 11.7 %cosine_convert_fusion = (bf16[2560,256]{1,0:T(8,128)(2,1)S(1)}, bf16[2560,256]{1,0:T(8,128)(2,1)S(1)}) fusion(s32[256]{0:T(256)S(1)} %compare_select_fusion, s32[2560]{0:T(1024)S(1)} %iota_add_fusion), kind=kLoop, calls=%fused_computation.34 | loop fusion | flops 11141120 | bytes 2632704 | tf_op jit(solution)/shard_map/convert.9
  190.5 74.7 %all-gather.2.cloned.1.call-done = bf16[512,2,2,2560]{3,2,1,0:T(2,128)(2,1)} async-done(((bf16[8,2,2,2560]{3,2,1,0:T(2,128)(2,1)}), bf16[512,2,2,2560]{3,2,1,0:T(2,128)(2,1)}) %all-gather.2.cloned.1.call-update) | async-done | bytes 10485776 | tf_op jit(solution)/shard_map/all_gather | solution.py:63
  265.2 13.0 %reshape.97 = bf16[64,81920]{1,0:T(8,128)(2,1)} reshape(bf16[512,2,2,2560]{3,2,1,0:T(2,128)(2,1)} %all-gather.2.cloned.1.call-done) | data formatting | bytes 20971520 | tf_op jit(solution)/shard_map/reshape | solution.py:64
  278.2 13.8 %dot_general.11 = bf16[8,2,2,2560,64]{3,2,1,0,4:T(2,128)(2,1)} reshape(bf16[81920,64]{0,1:T(8,128)(2,1)} %bitcast.71) | data formatting | bytes 20971520 | tf_op jit(solution)/shard_map/dot_general | solution.py:65
  292.0 16.1 %fusion.8 = f32[4,8,2,2,2560]{4,0,3,2,1:T(4,128)} fusion(bf16[8,2,2,2560,64]{3,2,1,0,4:T(2,128)(2,1)} %dot_general.11, s32[64]{0:T(128)S(1)} %add_reduce_fusion, pred[64]{0:T(512)(128)(4,1)S(1)} %fusion.14), kind=kOutput, calls=%fused_computation.19 | convolution fusion | flops 41943552 | bytes 11796800 | tf_op jit(solution)/shard_map/dot_general | solution.py:65
  308.2 51.6 %while.10 = (s32[]{:T(128)}, f32[4,8,128,256]{3,2,1,0:T(8,128)}, f32[4,8,2,2,2560]{4,0,3,2,1:T(4,128)}, bf16[2,128,2560]{2,1,0:T(8,128)(2,1)S(1)}, bf16[2,128,25...) while((s32[]{:T(128)}, f32[4,8,128,256]{3,2,1,0:T(8,128)}, ...), condition=%wide.region_4.5_spmd, body=%wide.region_3.4_spmd.sunk | while | flops 2748841984 | bytes 53281388 | solution.py:88
  311.3 5.8 %add_convert_fusion.2 = (bf16[8,128,2560]{2,1,0:T(8,128)(2,1)S(1)}, bf16[8,128,2560]{2,1,0:T(8,128)(2,1)S(1)}) fusion(f32[128,2560]{1,0:T(8,128)S(1)} %get-tuple-element.145, f32[8,2560]{1,0:T(8,128)S(1)} %get-tuple-element.148, f32[128,2560]{1,0:T(8,128)S(1)} %get-tuple-element.149, f32[8,2560]{1,0:T(8,128)S(1)} %get-tuple-element.150, ...), kind=kLoop, calls=%fused_computation.5.clone.1 | loop fusion | flops 41943040 | bytes 16056320 | tf_op jit(solution)/shard_map/convert.7
  317.1 3.1 fusion.29
  324.1 5.8 %add_convert_fusion.2 = (bf16[8,128,2560]{2,1,0:T(8,128)(2,1)S(1)}, bf16[8,128,2560]{2,1,0:T(8,128)(2,1)S(1)}) fusion(f32[128,2560]{1,0:T(8,128)S(1)} %get-tuple-element.145, f32[8,2560]{1,0:T(8,128)S(1)} %get-tuple-element.148, f32[128,2560]{1,0:T(8,128)S(1)} %get-tuple-element.149, f32[8,2560]{1,0:T(8,128)S(1)} %get-tuple-element.150, ...), kind=kLoop, calls=%fused_computation.5.clone.1 | loop fusion | flops 41943040 | bytes 16056320 | tf_op jit(solution)/shard_map/convert.7
  329.9 3.1 fusion.29
  336.9 5.8 %add_convert_fusion.2 = (bf16[8,128,2560]{2,1,0:T(8,128)(2,1)S(1)}, bf16[8,128,2560]{2,1,0:T(8,128)(2,1)S(1)}) fusion(f32[128,2560]{1,0:T(8,128)S(1)} %get-tuple-element.145, f32[8,2560]{1,0:T(8,128)S(1)} %get-tuple-element.148, f32[128,2560]{1,0:T(8,128)S(1)} %get-tuple-element.149, f32[8,2560]{1,0:T(8,128)S(1)} %get-tuple-element.150, ...), kind=kLoop, calls=%fused_computation.5.clone.1 | loop fusion | flops 41943040 | bytes 16056320 | tf_op jit(solution)/shard_map/convert.7
  342.7 3.1 fusion.29
  349.8 5.8 %add_convert_fusion.2 = (bf16[8,128,2560]{2,1,0:T(8,128)(2,1)S(1)}, bf16[8,128,2560]{2,1,0:T(8,128)(2,1)S(1)}) fusion(f32[128,2560]{1,0:T(8,128)S(1)} %get-tuple-element.145, f32[8,2560]{1,0:T(8,128)S(1)} %get-tuple-element.148, f32[128,2560]{1,0:T(8,128)S(1)} %get-tuple-element.149, f32[8,2560]{1,0:T(8,128)S(1)} %get-tuple-element.150, ...), kind=kLoop, calls=%fused_computation.5.clone.1 | loop fusion | flops 41943040 | bytes 16056320 | tf_op jit(solution)/shard_map/convert.7
  355.6 3.1 fusion.29
  359.8 94.6 %all-reduce.2.cloned.1.call-done = f32[4,8,128,256]{3,2,1,0:T(8,128)} async-done(((f32[4,8,128,256]{3,2,1,0:T(8,128)}), f32[4,8,128,256]{3,2,1,0:T(8,128)}) %all-reduce.2.cloned.1.call-update) | async-done | bytes 4194320 | tf_op jit(solution)/shard_map/psum | solution.py:89
  454.4 2.3 constant_dynamic-slice_fusion.1
  (60 shorter events, 21.1 us)
Async XLA Ops:
  6.5 258.7 %all-gather.2.cloned.1.call-start = ((), (), s32[]{:S(2)}) async-start(), calls=%async_computation | async-start | bytes 10649600 | tf_op jit(solution)/shard_map/all_gather | solution.py:63
  10.1 2.3 copy-start
  146.4 20.6 %copy-start.1 = (bf16[2,128,2560]{1,2,0:T(8,128)(2,1)}, bf16[2,128,2560]{1,2,0:T(8,128)(2,1)S(1)}, u32[]{:S(2)}) copy-start(bf16[2,128,2560]{1,2,0:T(8,128)(2,1)S(1)} %get-tuple-element.91) | copy-start | bytes 3932164
  174.4 280.0 %all-reduce.2.cloned.1.call-start = ((), (), s32[]{:S(2)}) async-start(), calls=%async_computation.1 | async-start | bytes 8388608 | tf_op jit(solution)/shard_map/psum | solution.py:89
  174.4 2.3 copy-start.3
  174.4 2.3 copy-start.4
  311.3 5.8 %copy-start.2 = (bf16[5120,256]{1,0:T(8,128)(2,1)S(1)}, bf16[5120,256]{1,0:T(8,128)(2,1)}, u32[]{:S(2)}) copy-start(bf16[5120,256]{1,0:T(8,128)(2,1)} %get-tuple-element.178) | copy-start | bytes 7864324 | tf_op jit(solution)/shard_map/while
  324.1 5.8 %copy-start.2 = (bf16[5120,256]{1,0:T(8,128)(2,1)S(1)}, bf16[5120,256]{1,0:T(8,128)(2,1)}, u32[]{:S(2)}) copy-start(bf16[5120,256]{1,0:T(8,128)(2,1)} %get-tuple-element.178) | copy-start | bytes 7864324 | tf_op jit(solution)/shard_map/while
  336.9 5.8 %copy-start.2 = (bf16[5120,256]{1,0:T(8,128)(2,1)S(1)}, bf16[5120,256]{1,0:T(8,128)(2,1)}, u32[]{:S(2)}) copy-start(bf16[5120,256]{1,0:T(8,128)(2,1)} %get-tuple-element.178) | copy-start | bytes 7864324 | tf_op jit(solution)/shard_map/while
  349.7 5.8 %copy-start.2 = (bf16[5120,256]{1,0:T(8,128)(2,1)S(1)}, bf16[5120,256]{1,0:T(8,128)(2,1)}, u32[]{:S(2)}) copy-start(bf16[5120,256]{1,0:T(8,128)(2,1)} %get-tuple-element.178) | copy-start | bytes 7864324 | tf_op jit(solution)/shard_map/while
Sparse Core Ops, SparseCore 0:
  174.5 90.6 all-gather.1
  359.9 94.4 all-reduce.1
where the time goes:
time: 467 us; the launch traced here: 464 us
  other arithmetic  178 us (38%)
  waiting for transfers between devices  169 us (36%)
  local copies, waits for them, and re-layouts  73.9 us (16%)
  matrix products  28.4 us (6%)
  between operations  14.1 us (3%)
    another operation x1, other arithmetic, whiten(): lax.reduce_window(amplitude, jnp.zeros((), amplitude.dtype), lax.add, win...  129 us
    psum x1, waiting for transfers between devices, shards(): summed_hours = lax.psum(partial_stacks, 'hour')  94.6 us
    all_gather x1, waiting for transfers between devices, shards(): gathered = lax.all_gather(local_sources, 'chan', axis=0, tiled=True)  74.7 us
    another operation x6, other arithmetic  34.9 us
    dot_general x1, matrix products, shards(): chosen = jnp.dot(onehot, flattened, preferred_element_type=jnp.float32)  16.1 us
    dot_general x1, local copies, waits for them, and re-layouts, shards(): chosen = jnp.dot(onehot, flattened, preferred_element_type=jnp.float32)  13.8 us
    reshape x1, local copies, waits for them, and re-layouts, shards(): flattened = gathered.reshape(block_count, -1)  13 us
    dot_general x4, matrix products, one_slot(): jnp.dot(cross, table_values, preferred_element_type=jnp.float32)  12.3 us
  transfers between devices with their start and end apart: 2, of which 2 were waited for; matrix products, arithmetic and copies ran while one was open for 3% of the time, Pallas kernels for 0%

commit v1 on v0

--- a/solution.py
+++ b/solution.py
@@ -86,7 +86,11 @@
         return lagged.reshape(VS, block_chans, LAGS)
 
     partial_stacks = lax.map(one_slot, chosen)
-    summed_hours = lax.psum(partial_stacks, "hour")
+    summed_hours = partial_stacks
+    for hop in (1, 2):
+        summed_hours = summed_hours + lax.ppermute(
+            summed_hours, "hour", [(dev, dev ^ hop) for dev in range(4)]
+        )
     share = slot_total // hour_count
     return lax.dynamic_slice_in_dim(summed_hours, lax.axis_index("hour") * share, share, 0)
 

time: 467 us -> 563 us (1.21)
  waiting for transfers between devices: 169 us -> 256 us
  other arithmetic: 178 us -> 185 us
    ppermute x0 -> x2, waiting for transfers between devices: none -> 181 us  [shards(): lax.ppermute(summed_hours, 'hour', [(dev, dev ^ hop) for dev in range(4)])]
    psum x1 -> x0, waiting for transfers between devices: 94.6 us -> none  [shards(): summed_hours = lax.psum(partial_stacks, 'hour')]
    add x0 -> x2, other arithmetic: none -> 7.5 us  [shards(): summed_hours + lax.ppermute(summed_hours, 'hour', [(dev, dev ^ hop) for d...]
  transfers between devices with their start and end apart: 2 -> 3, of which waited for: 2 -> 3; matrix products, arithmetic and copies ran while one was open for 3% -> 3% of each run, Pallas kernels for 0% -> 0%
where the time goes in v1:
time: 563 us; the launch traced here: 560 us
  waiting for transfers between devices  256 us (45%)
  other arithmetic  185 us (33%)
  local copies, waits for them, and re-layouts  71.6 us (13%)
  matrix products  28.4 us (5%)
  between operations  13.7 us (2%)
    ppermute x2, waiting for transfers between devices, shards(): lax.ppermute(summed_hours, 'hour', [(dev, dev ^ hop) for dev in range(4)])  181 us
    another operation x1, other arithmetic, whiten(): lax.reduce_window(amplitude, jnp.zeros((), amplitude.dtype), lax.add, win...  129 us
    all_gather x1, waiting for transfers between devices, shards(): gathered = lax.all_gather(local_sources, 'chan', axis=0, tiled=True)  74.8 us
    another operation x6, other arithmetic  34.9 us
    dot_general x1, matrix products, shards(): chosen = jnp.dot(onehot, flattened, preferred_element_type=jnp.float32)  16.1 us
    dot_general x1, local copies, waits for them, and re-layouts, shards(): chosen = jnp.dot(onehot, flattened, preferred_element_type=jnp.float32)  13.8 us
    reshape x1, local copies, waits for them, and re-layouts, shards(): flattened = gathered.reshape(block_count, -1)  13 us
    dot_general x4, matrix products, one_slot(): jnp.dot(cross, table_values, preferred_element_type=jnp.float32)  12.3 us
  transfers between devices with their start and end apart: 3, of which 3 were waited for; matrix products, arithmetic and copies ran while one was open for 3% of the time, Pallas kernels for 0%

profile of v1, /device:TPU:1, one launch (start us, length us, event | category | flops | bytes accessed | tf_op | source)
XLA Modules:
  0.0 559.6 jit_solution(15308878324689433575)
XLA Ops:
  6.5 3.2 copy.26
  13.3 129.3 %reduce_window.7 = f32[2,128,2560]{1,2,0:T(8,128)} reduce-window(f32[2,128,2560]{1,2,0:T(8,128)S(1)} %add_sqrt_fusion, f32[]{:T(128)} %constant.29.clone.1), window={size=1x1x129 pad=0_0x0_0x64_64}, to_apply=%region_2.0 | reduce-window | flops 83886080 | bytes 5242884 | tf_op jit(solution)/shard_map/reduce_window | solution.py:18
  142.6 4.0 divide_convert_fusion.1
  146.6 10.4 %slice.38 = bf16[2,8,2560]{1,2,0:T(8,128)(2,1)} slice(bf16[2,128,2560]{1,2,0:T(8,128)(2,1)S(1)} %get-tuple-element.90), slice={[0:2:1], [0:128:16], [0:2560:1]} | slice | bytes 163840 | tf_op jit(solution)/shard_map/slice | solution.py:58
  157.0 10.2 %slice.39 = bf16[2,8,2560]{1,2,0:T(8,128)(2,1)} slice(bf16[2,128,2560]{1,2,0:T(8,128)(2,1)S(1)} %get-tuple-element.91), slice={[0:2:1], [0:128:16], [0:2560:1]} | slice | bytes 163840 | tf_op jit(solution)/shard_map/slice | solution.py:58
  167.2 3.8 maximum_bitcast_fusion
  171.1 3.5 copy.27
  177.3 11.7 %cosine_convert_fusion = (bf16[2560,256]{1,0:T(8,128)(2,1)S(1)}, bf16[2560,256]{1,0:T(8,128)(2,1)S(1)}) fusion(s32[256]{0:T(256)S(1)} %compare_select_fusion, s32[2560]{0:T(1024)S(1)} %iota_add_fusion), kind=kLoop, calls=%fused_computation.34 | loop fusion | flops 11141120 | bytes 2632704 | tf_op jit(solution)/shard_map/convert.9
  190.7 74.8 %all-gather.2.cloned.1.call-done = bf16[512,2,2,2560]{3,2,1,0:T(2,128)(2,1)} async-done(((bf16[8,2,2,2560]{3,2,1,0:T(2,128)(2,1)}), bf16[512,2,2,2560]{3,2,1,0:T(2,128)(2,1)}) %all-gather.2.cloned.1.call-update) | async-done | bytes 10485776 | tf_op jit(solution)/shard_map/all_gather | solution.py:63
  265.5 13.0 %reshape.97 = bf16[64,81920]{1,0:T(8,128)(2,1)} reshape(bf16[512,2,2,2560]{3,2,1,0:T(2,128)(2,1)} %all-gather.2.cloned.1.call-done) | data formatting | bytes 20971520 | tf_op jit(solution)/shard_map/reshape | solution.py:64
  278.4 13.8 %dot_general.11 = bf16[8,2,2,2560,64]{3,2,1,0,4:T(2,128)(2,1)} reshape(bf16[81920,64]{0,1:T(8,128)(2,1)} %bitcast.71) | data formatting | bytes 20971520 | tf_op jit(solution)/shard_map/dot_general | solution.py:65
  292.3 16.1 %fusion.8 = f32[4,8,2,2,2560]{4,0,3,2,1:T(4,128)} fusion(bf16[8,2,2,2560,64]{3,2,1,0,4:T(2,128)(2,1)} %dot_general.11, s32[64]{0:T(128)S(1)} %add_reduce_fusion, pred[64]{0:T(512)(128)(4,1)S(1)} %fusion.14), kind=kOutput, calls=%fused_computation.19 | convolution fusion | flops 41943552 | bytes 11796800 | tf_op jit(solution)/shard_map/dot_general | solution.py:65
  308.4 51.7 %while.10 = (s32[]{:T(128)}, f32[4,8,128,256]{3,2,1,0:T(8,128)}, f32[4,8,2,2,2560]{4,0,3,2,1:T(4,128)}, bf16[2,128,2560]{2,1,0:T(8,128)(2,1)S(1)}, bf16[2,128,25...) while((s32[]{:T(128)}, f32[4,8,128,256]{3,2,1,0:T(8,128)}, ...), condition=%wide.region_4.5_spmd, body=%wide.region_3.4_spmd.sunk | while | flops 2748841984 | bytes 53281388 | solution.py:88
  311.7 5.8 %add_convert_fusion.2 = (bf16[8,128,2560]{2,1,0:T(8,128)(2,1)S(1)}, bf16[8,128,2560]{2,1,0:T(8,128)(2,1)S(1)}) fusion(f32[128,2560]{1,0:T(8,128)S(1)} %get-tuple-element.145, f32[8,2560]{1,0:T(8,128)S(1)} %get-tuple-element.148, f32[128,2560]{1,0:T(8,128)S(1)} %get-tuple-element.149, f32[8,2560]{1,0:T(8,128)S(1)} %get-tuple-element.150, ...), kind=kLoop, calls=%fused_computation.5.clone.1 | loop fusion | flops 41943040 | bytes 16056320 | tf_op jit(solution)/shard_map/convert.7
  317.5 3.1 fusion.29
  324.5 5.8 %add_convert_fusion.2 = (bf16[8,128,2560]{2,1,0:T(8,128)(2,1)S(1)}, bf16[8,128,2560]{2,1,0:T(8,128)(2,1)S(1)}) fusion(f32[128,2560]{1,0:T(8,128)S(1)} %get-tuple-element.145, f32[8,2560]{1,0:T(8,128)S(1)} %get-tuple-element.148, f32[128,2560]{1,0:T(8,128)S(1)} %get-tuple-element.149, f32[8,2560]{1,0:T(8,128)S(1)} %get-tuple-element.150, ...), kind=kLoop, calls=%fused_computation.5.clone.1 | loop fusion | flops 41943040 | bytes 16056320 | tf_op jit(solution)/shard_map/convert.7
  330.3 3.1 fusion.29
  337.3 5.8 %add_convert_fusion.2 = (bf16[8,128,2560]{2,1,0:T(8,128)(2,1)S(1)}, bf16[8,128,2560]{2,1,0:T(8,128)(2,1)S(1)}) fusion(f32[128,2560]{1,0:T(8,128)S(1)} %get-tuple-element.145, f32[8,2560]{1,0:T(8,128)S(1)} %get-tuple-element.148, f32[128,2560]{1,0:T(8,128)S(1)} %get-tuple-element.149, f32[8,2560]{1,0:T(8,128)S(1)} %get-tuple-element.150, ...), kind=kLoop, calls=%fused_computation.5.clone.1 | loop fusion | flops 41943040 | bytes 16056320 | tf_op jit(solution)/shard_map/convert.7
  343.1 3.1 fusion.29
  350.2 5.8 %add_convert_fusion.2 = (bf16[8,128,2560]{2,1,0:T(8,128)(2,1)S(1)}, bf16[8,128,2560]{2,1,0:T(8,128)(2,1)S(1)}) fusion(f32[128,2560]{1,0:T(8,128)S(1)} %get-tuple-element.145, f32[8,2560]{1,0:T(8,128)S(1)} %get-tuple-element.148, f32[128,2560]{1,0:T(8,128)S(1)} %get-tuple-element.149, f32[8,2560]{1,0:T(8,128)S(1)} %get-tuple-element.150, ...), kind=kLoop, calls=%fused_computation.5.clone.1 | loop fusion | flops 41943040 | bytes 16056320 | tf_op jit(solution)/shard_map/convert.7
  356.0 3.1 fusion.29
  361.4 90.9 %collective-permute-done = f32[4,8,128,256]{3,2,1,0:T(8,128)S(1)} collective-permute-done((f32[4,8,128,256]{3,2,1,0:T(8,128)}, f32[4,8,128,256]{3,2,1,0:T(8,128)S(1)}, u32[]{:S(2)}, u32[]{:S(2)}) %collective-permute-start) | collective-permute-done | bytes 4194336 | tf_op jit(solution)/shard_map/ppermute | solution.py:91
  452.3 4.9 add.101
  459.9 90.1 %collective-permute-done.1 = f32[4,8,128,256]{3,2,1,0:T(8,128)} collective-permute-done((f32[4,8,128,256]{3,2,1,0:T(8,128)}, f32[4,8,128,256]{3,2,1,0:T(8,128)}, u32[]{:S(2)}, u32[]{:S(2)}) %collective-permute-start.1) | collective-permute-done | bytes 4194336 | tf_op jit(solution)/shard_map/ppermute | solution.py:91
  (62 shorter events, 29.9 us)
Async XLA Ops:
  6.5 258.9 %all-gather.2.cloned.1.call-start = ((), (), s32[]{:S(2)}) async-start(), calls=%async_computation | async-start | bytes 10649600 | tf_op jit(solution)/shard_map/all_gather | solution.py:63
  10.1 2.3 copy-start
  146.6 20.7 %copy-start.1 = (bf16[2,128,2560]{1,2,0:T(8,128)(2,1)}, bf16[2,128,2560]{1,2,0:T(8,128)(2,1)S(1)}, u32[]{:S(2)}) copy-start(bf16[2,128,2560]{1,2,0:T(8,128)(2,1)S(1)} %get-tuple-element.91) | copy-start | bytes 3932164
  174.6 2.3 copy-start.3
  174.6 2.3 copy-start.4
  311.7 5.8 %copy-start.2 = (bf16[5120,256]{1,0:T(8,128)(2,1)S(1)}, bf16[5120,256]{1,0:T(8,128)(2,1)}, u32[]{:S(2)}) copy-start(bf16[5120,256]{1,0:T(8,128)(2,1)} %get-tuple-element.178) | copy-start | bytes 7864324 | tf_op jit(solution)/shard_map/while
  324.5 5.8 %copy-start.2 = (bf16[5120,256]{1,0:T(8,128)(2,1)S(1)}, bf16[5120,256]{1,0:T(8,128)(2,1)}, u32[]{:S(2)}) copy-start(bf16[5120,256]{1,0:T(8,128)(2,1)} %get-tuple-element.178) | copy-start | bytes 7864324 | tf_op jit(solution)/shard_map/while
  337.3 5.8 %copy-start.2 = (bf16[5120,256]{1,0:T(8,128)(2,1)S(1)}, bf16[5120,256]{1,0:T(8,128)(2,1)}, u32[]{:S(2)}) copy-start(bf16[5120,256]{1,0:T(8,128)(2,1)} %get-tuple-element.178) | copy-start | bytes 7864324 | tf_op jit(solution)/shard_map/while
  350.1 5.8 %copy-start.2 = (bf16[5120,256]{1,0:T(8,128)(2,1)S(1)}, bf16[5120,256]{1,0:T(8,128)(2,1)}, u32[]{:S(2)}) copy-start(bf16[5120,256]{1,0:T(8,128)(2,1)} %get-tuple-element.178) | copy-start | bytes 7864324 | tf_op jit(solution)/shard_map/while
  360.2 92.1 %collective-permute-start = (f32[4,8,128,256]{3,2,1,0:T(8,128)}, f32[4,8,128,256]{3,2,1,0:T(8,128)S(1)}, u32[]{:S(2)}, u32[]{:S(2)}) collective-permute-start(f32[4,8,128,256]{3,2,1,0:T(8,128)} %get-tuple-element.37), channel_id=1, source_target_pairs={{0,1},{1,0},{2,3},{3,2},{4,5},{5,4},{6,7},{7,6},{8,9},{9,8},{10,11... | collective-permute-start | bytes 12582920 | tf_op jit(solution)/shard_map/ppermute | solution.py:91
  457.1 92.8 %collective-permute-start.1 = (f32[4,8,128,256]{3,2,1,0:T(8,128)}, f32[4,8,128,256]{3,2,1,0:T(8,128)}, u32[]{:S(2)}, u32[]{:S(2)}) collective-permute-start(f32[4,8,128,256]{3,2,1,0:T(8,128)} %add.101), channel_id=1, source_target_pairs={{0,2},{1,3},{2,0},{3,1},{4,6},{5,7},{6,4},{7,5},{8,10},{9,11},{10,... | collective-permute-start | bytes 12582920 | tf_op jit(solution)/shard_map/ppermute | solution.py:91
Sparse Core Ops, SparseCore 0:
  174.7 90.6 all-gather.1
